TPU v7x, 32 devices: a whole 2x2x4 slice. The times are simulated.
32 devices in a mesh: tm: 4 (over y, x), aux: 4 (over z), pair: 2 (over core).
Axes of the slice: x: 2, y: 2, z: 4, core: 2. Of those that a mesh axis runs over, the one named last changes fastest.
Arguments:
- factors: bfloat16 [3072, 5120], P('aux', 'pair'), may hold values from -0.078125 to 0.078125
- panel_factors: bfloat16 [256, 5120], P('aux', 'pair'), may hold values from -6 to 6
- time_weights: float32 [12, 5120], P('tm', 'pair'), may hold values from 0.2 to 2
- tile_mask: int32 [24, 40], P('aux', 'pair'), may hold values 0 or 1
- forward_table: float32 [12, 12], replicated, may hold values from -0.5 to 0.5
- screening: float32 [12, 256, 256], P('tm', 'aux'), may hold values from -0.375 to 0.375
- back_table: float32 [12, 12], replicated, may hold values from -0.5 to 0.5
Outputs:
- sigma: float32 [12, 5120], P('tm', 'pair')
All inputs are finite; a program needn't handle non-finite values. No bound on the sum of `tile_mask` on one device may be relied on, other than what follows from the above.
Results may differ from a plain program's by a relative error of at most 0.0003.
Values may be sent and summed in bfloat16 or wider, within the bound.
No kernel may reach another device: no remote copies, remote signals or barrier semaphores. Data moves between devices by JAX's collectives and lax.ppermute only.
A program may use at most 64 MiB of HBM per device.

v0:
```python
import jax
import jax.numpy as jnp
from jax import lax
from jax.sharding import PartitionSpec as P

TILE = 128


def expand_tiles(tile_mask):
    tile_rows, tile_cols = tile_mask.shape
    spread = jnp.broadcast_to(tile_mask[:, None, :, None], (tile_rows, TILE, tile_cols, TILE))
    return spread.reshape(tile_rows * TILE, tile_cols * TILE)


def body(factors, panel_factors, time_weights, tile_mask, forward_table, screening, back_table):
    highest = lax.Precision.HIGHEST
    masked = factors.astype(jnp.float32) * expand_tiles(tile_mask).astype(jnp.float32)
    panel_full = lax.all_gather(panel_factors, "aux", axis=0, tiled=True)
    panel_wide = panel_full.astype(jnp.float32)
    freq_count = screening.shape[0]
    first_freq = lax.axis_index("tm") * freq_count
    weights_all = lax.all_gather(time_weights, "tm", axis=0, tiled=True)
    table_rows = lax.dynamic_slice_in_dim(forward_table, first_freq, freq_count, 0)
    line_weights = jnp.dot(table_rows, weights_all, precision=highest)
    scaled = panel_wide[None, :, :] * line_weights[:, None, :]
    polar_line = jnp.einsum("tpk,qk->tpq", scaled, masked, precision=highest)
    polar_half = lax.psum_scatter(polar_line, "pair", scatter_dimension=2, tiled=True)
    inverse = lax.all_gather(screening, "aux", axis=1, tiled=True)
    screened = jnp.einsum("wpr,wrq->wpq", inverse, polar_half, precision=highest)
    back_cols = lax.dynamic_slice_in_dim(back_table, first_freq, freq_count, 1)
    lines_full = lax.all_gather(screened, "pair", axis=2, tiled=True)
    contracted = jnp.einsum("tpq,qk->tpk", lines_full, masked, precision=highest)
    partial_value = jnp.sum(panel_wide[None, :, :] * contracted, axis=1) * panel_full.shape[0] ** (
        -0.5
    )
    timed = jnp.dot(back_cols, partial_value, precision=highest)
    partial_value = lax.psum_scatter(timed, "tm", scatter_dimension=0, tiled=True)
    return lax.psum(partial_value, "aux")


def solution(mesh):
    placed = (
        P("aux", "pair"),
        P("aux", "pair"),
        P("tm", "pair"),
        P("aux", "pair"),
        P(),
        P("tm", "aux", None),
        P(),
    )
    return jax.shard_map(
        body, mesh=mesh, in_specs=placed, out_specs=P("tm", "pair"), check_vma=False
    )
```

profile of v0, /device:TPU:0, one launch (start us, length us, event | category | flops | bytes accessed | tf_op | source)
XLA Modules:
  0.0 203.3 jit_solution(14828435998711935432)
XLA Ops:
  6.5 0.0 copy-start
  6.5 0.0 all-gather.4.cloned.1.call-start
  6.5 0.7 all-gather.4.cloned.1.call-update
  7.3 0.0 reduce-scatter.2.cloned.1.call-start
  7.3 10.3 %all-gather = f32[4,3,2560]{2,1,0:T(4,128)S(1)} all-gather(f32[1,3,2560]{2,1,0:T(4,128)} %bitcast.22), channel_id=1, replica_groups=mesh['tm'=4,'aux'=4,'pair'=2] {'tm'}, dimensions={0}, use_global_device_ids=true | all-gather | bytes 153600 | tf_op jit(solution)/shard_map/all_gather | solution.py:22
  17.6 0.1 reshape.6
  17.7 0.7 convert_element_type.15
  18.4 0.9 fusion.11
  19.3 24.9 %all-gather.4.cloned.1.call-done = bf16[256,2560]{1,0:T(8,128)(2,1)} async-done(((bf16[64,2560]{1,0:T(8,128)(2,1)}), bf16[256,2560]{1,0:T(8,128)(2,1)}) %all-gather.4.cloned.1.call-update) | async-done | bytes 1310736 | tf_op jit(solution)/shard_map/all_gather | solution.py:18
  44.2 1.6 convert_element_type.13
  45.8 0.0 copy-start.2
  45.8 0.7 broadcast_in_dim.2
  46.5 0.0 copy-start.1
  46.5 3.7 %copy-done.1 = f32[6,128,20,128]{3,2,1,0:T(8,128)} copy-done((f32[6,128,20,128]{3,2,1,0:T(8,128)}, f32[6,128,20,128]{3,2,1,0:T(8,128)S(1)}, u32[]{:S(2)}) %copy-start.1) | copy-done | bytes 7864344
  50.2 0.0 copy-done.2
  50.2 22.1 %fusion.1 = f32[3,256,768]{2,1,0:T(8,128)} fusion(f32[96,8,20,128]{3,2,1,0:T(8,128)S(1)} %bitcast.20, bf16[768,2560]{1,0:T(8,128)(2,1)S(1)} %copy-done.2, f32[3,2560]{1,0:T(4,128)S(1)} %fusion.11, f32[256,2560]{1,0:T(8,128)S(1)} %convert_element_type.13), kind=kOutput, calls=%fused_computation.3 | convolution fusion | flops 18125291520 | bytes 16807936 | tf_op jit(solution)/shard_map/tpk,qk->tpq/dot_general | solution.py:26
  72.3 0.0 reduce-scatter.2.cloned.1.call-update
  72.3 0.0 all-gather.6.cloned.1.call-start
  72.4 18.2 %all_gather.14 = f32[3,256,256]{2,1,0:T(8,128)S(1)} all-gather(f32[3,64,256]{2,1,0:T(8,128)} %param.12), channel_id=1, replica_groups=mesh['tm'=4,'aux'=4,'pair'=2] {'aux'}, dimensions={1}, use_global_device_ids=true | all-gather | bytes 983040 | tf_op jit(solution)/shard_map/all_gather | solution.py:28
  90.6 0.0 reduce-scatter.2.cloned.1.call-done
  90.6 4.4 %convolution_bitcast_fusion = f32[3,256,384]{1,2,0:T(8,128)} fusion(f32[3,256,384]{2,1,0:T(8,128)} %reduce-scatter.2.cloned.1.call-done, f32[3,256,256]{2,1,0:T(8,128)S(1)} %all_gather.14), kind=kOutput, calls=%fused_computation.7 | convolution fusion | flops 905969664 | bytes 3145728 | tf_op jit(solution)/shard_map/wpr,wrq->wpq/dot_general | solution.py:29
  94.9 0.0 all-gather.6.cloned.1.call-update
  95.0 0.0 copy-start.3
  95.0 0.0 all-reduce.3.cloned.1.call-start
  95.0 10.5 %all-gather.6.cloned.1.call-done = f32[3,256,768]{1,2,0:T(8,128)} async-done(((f32[3,256,384]{1,2,0:T(8,128)}), f32[3,256,768]{1,2,0:T(8,128)}) %all-gather.6.cloned.1.call-update) | async-done | bytes 2359312 | tf_op jit(solution)/shard_map/all_gather | solution.py:31
  105.5 25.5 %multiply_reduce_fusion = f32[3,2560]{1,0:T(4,128)S(1)} fusion(f32[3,256,768]{1,2,0:T(8,128)} %all-gather.6.cloned.1.call-done, f32[96,8,20,128]{3,2,1,0:T(8,128)} %bitcast.21, bf16[768,2560]{1,0:T(8,128)(2,1)} %param.7, f32[256,2560]{1,0:T(8,128)S(1)} %convert_element_type.13), kind=kOutput, calls=%fused_computation.2 | convolution fusion | flops 18127249408 | bytes 16807936 | tf_op jit(solution)/shard_map/tpq,qk->tpk/dot_general | solution.py:32
  131.1 0.0 copy-done
  131.1 1.0 fusion.7
  132.1 0.0 all-reduce.3.cloned.1.call-update
  132.1 0.0 copy-done.3
  132.1 0.6 dynamic-slice
  133.4 42.5 %all-reduce.3.cloned.1.call-done = f32[12,2560]{1,0:T(8,128)} async-done(((f32[12,2560]{1,0:T(8,128)}), f32[12,2560]{1,0:T(8,128)}) %all-reduce.3.cloned.1.call-update) | async-done | bytes 122896
  175.9 0.9 constant_dynamic-slice_fusion
  176.8 20.0 %psum.7 = f32[3,2560]{1,0:T(4,128)} all-reduce(f32[3,2560]{1,0:T(4,128)S(1)} %constant_dynamic-slice_fusion), channel_id=1, replica_groups=mesh['tm'=4,'aux'=4,'pair'=2] {'aux'}, use_global_device_ids=true, to_apply=%region_3.0 | all-reduce | flops 7680 | bytes 61440 | tf_op jit(solution)/shard_map/psum | solution.py:38
Async XLA Ops:
  6.5 124.5 %copy-start = (f32[12,12]{1,0:T(8,128)S(1)}, f32[12,12]{1,0:T(8,128)}, u32[]{:S(2)}) copy-start(f32[12,12]{1,0:T(8,128)} %param.13) | copy-start | bytes 1732
  6.5 37.7 %all-gather.4.cloned.1.call-start = ((), (), s32[]{:S(2)}) async-start(), calls=%async_computation.1 | async-start | bytes 1638400 | tf_op jit(solution)/shard_map/all_gather | solution.py:18
  7.3 83.3 %reduce-scatter.2.cloned.1.call-start = ((), (), s32[]{:S(2)}) async-start(), calls=%async_computation.2 | async-start | bytes 3538944 | tf_op jit(solution)/shard_map/reduce_scatter | solution.py:27
  45.8 4.4 %copy-start.2 = (bf16[768,2560]{1,0:T(8,128)(2,1)S(1)}, bf16[768,2560]{1,0:T(8,128)(2,1)}, u32[]{:S(2)}) copy-start(bf16[768,2560]{1,0:T(8,128)(2,1)} %param.7) | copy-start | bytes 11796484
  46.5 3.7 %copy-start.1 = (f32[6,128,20,128]{3,2,1,0:T(8,128)}, f32[6,128,20,128]{3,2,1,0:T(8,128)S(1)}, u32[]{:S(2)}) copy-start(f32[6,128,20,128]{3,2,1,0:T(8,128)S(1)} %broadcast_in_dim.2) | copy-start | bytes 23592964
  72.3 33.2 %all-gather.6.cloned.1.call-start = ((), (), s32[]{:S(2)}) async-start(), calls=%async_computation.3 | async-start | bytes 3538944 | tf_op jit(solution)/shard_map/all_gather | solution.py:31
  95.0 37.2 %copy-start.3 = (u32[32]{0:T(128)S(1)}, u32[32]{0:T(128)}, u32[]{:S(2)}) copy-start(u32[32]{0:T(128)} %constant.20) | copy-start | bytes 388
  95.0 80.9 %all-reduce.3.cloned.1.call-start = ((), (), s32[]{:S(2)}) async-start(), calls=%async_computation.4 | async-start | bytes 327680
Sparse Core Ops, SparseCore 0:
  8.9 35.2 all-gather.3
  72.5 9.0 reduce-scatter.1
  95.1 10.3 all-gather.5
  132.2 43.6 all-reduce.2
where the time goes:
time: 204 us; the launch traced here: 203 us
  waiting for transfers between devices  78.7 us (39%)
  matrix products  53.9 us (26%)
  blocking collectives  48.5 us (24%)
  between operations  13.9 us (7%)
  local copies, waits for them, and re-layouts  5.96 us (3%)
  other arithmetic  2.31 us (1%)
    unnamed x5, waiting for transfers between devices  43.3 us
    dot_general x1, matrix products, body(): jnp.einsum('tpq,qk->tpk', lines_full, masked, precision=highest)  25.5 us
    all_gather x1, waiting for transfers between devices, body(): panel_full = lax.all_gather(panel_factors, 'aux', axis=0, tiled=True)  24.9 us
    dot_general x1, matrix products, body(): polar_line = jnp.einsum('tpk,qk->tpq', scaled, masked, precision=highest)  22.1 us
    psum x1, blocking collectives, body(): return lax.psum(partial_value, 'aux')  20 us
    all_gather x1, blocking collectives, body(): inverse = lax.all_gather(screening, 'aux', axis=1, tiled=True)  18.2 us
    all_gather x1, waiting for transfers between devices, body(): lines_full = lax.all_gather(screened, 'pair', axis=2, tiled=True)  10.5 us
    all_gather x1, blocking collectives, body(): weights_all = lax.all_gather(time_weights, 'tm', axis=0, tiled=True)  10.3 us
  transfers between devices with their start and end apart: 4, of which 3 were waited for; matrix products, arithmetic and copies ran while one was open for 1% of the time, Pallas kernels for 0%

commit v1 on v0

v1 whole, which is shorter than its diff:
```python
import functools

import jax
import jax.numpy as jnp
from jax import lax
from jax.experimental import pallas as pl
from jax.experimental.pallas import tpu as pltpu
from jax.sharding import PartitionSpec as P

TILE = 128
F8 = jnp.float8_e4m3fn
BF = jnp.bfloat16
F32 = jnp.float32
TOP = 256.0
TINY = 1e-30
SMEM = pltpu.MemorySpace.SMEM
VMEM = pltpu.MemorySpace.VMEM


def dot_nt(a, b):
    return lax.dot_general(a, b, (((1,), (1,)), ((), ())), preferred_element_type=F32)


def dot_nn(a, b):
    return lax.dot_general(a, b, (((1,), (0,)), ((), ())), preferred_element_type=F32)


def swap_with(value, axis, step, size):
    return lax.ppermute(value, axis, [(at, at ^ step) for at in range(size)])


def cost(flops, nbytes):
    return pl.CostEstimate(flops=int(flops), bytes_accessed=int(nbytes), transcendentals=0)


def mask_kernel(tile_ref, factors_ref, wide_ref, narrow_ref, scale_ref):
    rows, cols = factors_ref.shape
    top = jnp.zeros((TILE, TILE), F32)
    for col in range(0, cols, TILE):
        for row in range(0, rows, TILE):
            top = jnp.maximum(top, jnp.abs(factors_ref[row : row + TILE, col : col + TILE].astype(F32)))
    scale = TOP / jnp.maximum(jnp.max(top), TINY)
    scale_ref[0] = 1.0 / scale
    for col in range(0, cols, TILE):
        for row in range(0, rows, TILE):
            keep = tile_ref[row // TILE, col // TILE].astype(F32)
            block = factors_ref[row : row + TILE, col : col + TILE].astype(F32) * keep
            wide_ref[row : row + TILE, col : col + TILE] = block.astype(BF)
            narrow_ref[row : row + TILE, col : col + TILE] = (block * scale).astype(F8)


def mask_factors(tile_mask, factors):
    vmem = pl.BlockSpec(memory_space=VMEM)
    smem = pl.BlockSpec(memory_space=SMEM)
    return pl.pallas_call(
        mask_kernel,
        name="mask",
        in_specs=[smem, vmem],
        out_specs=[vmem, vmem, smem],
        out_shape=[
            jax.ShapeDtypeStruct(factors.shape, BF),
            jax.ShapeDtypeStruct(factors.shape, F8),
            jax.ShapeDtypeStruct((1,), F32),
        ],
        compiler_params=pltpu.CompilerParams(vmem_limit_bytes=24 << 20),
        cost_estimate=cost(4 * factors.size, 5 * factors.size),
    )(tile_mask, factors)


def combine_kernel(factor, count, at_ref, table_ref, *refs):
    blocks, out_ref = refs[:-1], refs[-1]
    me = at_ref[0]
    size = blocks[0].shape[0]
    total = [None] * count
    for step, block_ref in enumerate(blocks):
        first = (me ^ step) * size
        for line in range(size):
            values = block_ref[line : line + 1, :]
            for row in range(count):
                term = values * table_ref[me * count + row, first + line]
                total[row] = term if total[row] is None else total[row] + term
    for row in range(count):
        out_ref[row : row + 1, :] = total[row] * factor if factor != 1.0 else total[row]


def combine(at, table, blocks, count, factor, name):
    vmem = pl.BlockSpec(memory_space=VMEM)
    smem = pl.BlockSpec(memory_space=SMEM)
    return pl.pallas_call(
        functools.partial(combine_kernel, factor, count),
        name=name,
        in_specs=[smem, smem] + [vmem] * len(blocks),
        out_specs=vmem,
        out_shape=jax.ShapeDtypeStruct((count, blocks[0].shape[1]), F32),
        compiler_params=pltpu.CompilerParams(vmem_limit_bytes=8 << 20),
        cost_estimate=cost(100 * blocks[0].size, 4 * blocks[0].size * (len(blocks) + 1)),
    )(at, table, *blocks)


def polar_kernel(n_pieces, scale_ref, weights_ref, *refs):
    pieces = refs[:n_pieces]
    wide_ref, narrow_ref, out_ref, high, low = refs[n_pieces:]
    lines = weights_ref.shape[0]
    rows = high.shape[0] // lines

    @pl.when(pl.program_id(0) == 0)
    def _():
        out_ref[...] = jnp.zeros_like(out_ref)

    unscale = scale_ref[0]
    for line in range(lines):
        weight = weights_ref[line : line + 1, :]
        bound = jnp.max(jnp.abs(weight), axis=1, keepdims=True) * (1.0 / 256.0)
        backs = []
        at = line * rows
        for piece_ref in pieces:
            step = 32
            for start in range(0, piece_ref.shape[0], step):
                value = piece_ref[start : start + step, :].astype(F32)
                top = jnp.maximum(jnp.max(jnp.abs(value), axis=1, keepdims=True) * bound, TINY)
                back = top * (1.0 / TOP)
                value = value * weight
                rounded = value.astype(BF)
                high[at : at + step, :] = rounded
                low[at : at + step, :] = ((value - rounded.astype(F32)) * (1.0 / back)).astype(F8)
                backs.append(back * unscale)
                at += step
        span = slice(line * rows, (line + 1) * rows)
        back = jnp.concatenate(backs, axis=0)
        out_ref[span, :] += dot_nt(high[span, :], wide_ref[...]) + dot_nt(low[span, :], narrow_ref[...]) * back


def polar(scale, weights, pieces, wide, narrow, name, chunk=512):
    lines, depth = weights.shape
    rows = lines * sum(piece.shape[0] for piece in pieces)
    aux = wide.shape[0]
    part = lambda n: pl.BlockSpec((n, chunk), lambda k: (0, k))
    return pl.pallas_call(
        functools.partial(polar_kernel, len(pieces)),
        name=name,
        grid=(depth // chunk,),
        in_specs=[pl.BlockSpec(memory_space=SMEM), part(lines)]
        + [part(piece.shape[0]) for piece in pieces]
        + [part(aux), part(aux)],
        out_specs=pl.BlockSpec((rows, aux), lambda k: (0, 0)),
        out_shape=jax.ShapeDtypeStruct((rows, aux), F32),
        scratch_shapes=[pltpu.VMEM((rows, chunk), BF), pltpu.VMEM((rows, chunk), F8)],
        compiler_params=pltpu.CompilerParams(vmem_limit_bytes=24 << 20),
        cost_estimate=cost(3 * rows * aux * depth, 3 * aux * depth + 4 * rows * aux),
    )(scale, weights, *pieces, wide, narrow)


def split_rows(mine, other, high, low, back):
    step = 32
    for start in range(0, mine.shape[0], step):
        span = slice(start, start + step)
        value = mine[span, :] + other[span, :]
        rounded = value.astype(BF)
        rest = value - rounded.astype(F32)
        top = jnp.maximum(jnp.max(jnp.abs(rest), axis=1, keepdims=True), TINY) * (1.0 / TOP)
        high[span, :] = rounded
        low[span, :] = (rest * (1.0 / top)).astype(F8)
        back[span, :] = jnp.broadcast_to(top, (step, back.shape[1]))


def spread_kernel(scale_ref, mine_ref, other_ref, wide_ref, narrow_ref, out_ref, high, low, back):
    @pl.when(pl.program_id(0) == 0)
    def _():
        split_rows(mine_ref, other_ref, high, low, back)

    unscale = back[:, 0:1] * scale_ref[0]
    out_ref[...] = dot_nn(high[...], wide_ref[...]) + dot_nn(low[...], narrow_ref[...]) * unscale


def spread(scale, mine, other, wide, narrow, name, chunk=512):
    rows, aux = mine.shape
    depth = wide.shape[1]
    part = lambda n: pl.BlockSpec((n, chunk), lambda k: (0, k))
    whole = lambda shape: pl.BlockSpec(shape, lambda k: (0, 0))
    return pl.pallas_call(
        spread_kernel,
        name=name,
        grid=(depth // chunk,),
        in_specs=[pl.BlockSpec(memory_space=SMEM), whole((rows, aux)), whole((rows, aux)), part(aux), part(aux)],
        out_specs=part(rows),
        out_shape=jax.ShapeDtypeStruct((rows, depth), F32),
        scratch_shapes=[
            pltpu.VMEM((rows, aux), BF),
            pltpu.VMEM((rows, aux), F8),
            pltpu.VMEM((rows, TILE), F32),
        ],
        compiler_params=pltpu.CompilerParams(vmem_limit_bytes=24 << 20),
        cost_estimate=cost(3 * rows * aux * depth, 3 * aux * depth + 4 * rows * (aux + depth)),
    )(scale, mine, other, wide, narrow)


def close_kernel(layout, groups, n_screen, at_ref, scale_ref, mine_ref, other_ref, wide_ref, narrow_ref, *refs):
    pieces = refs[: len(layout)]
    screens = refs[len(layout) : len(layout) + n_screen]
    done = refs[len(layout) + n_screen : len(layout) + n_screen + len(groups) - 1]
    out_ref, high, low, back, square, turned, rest, panel, folded, last = refs[len(layout) + n_screen + len(groups) - 1 :]
    lines, total = square.shape[0], square.shape[1]

    @pl.when(pl.program_id(0) == 0)
    def _():
        split_rows(mine_ref, other_ref, high, low, back)
        for line in range(lines):
            for which, screen_ref in enumerate(screens):
                size = screen_ref.shape[1]
                first = pl.multiple_of(at_ref[which] * size, size)
                square[line, pl.ds(first, size), :] = screen_ref[line]
            flipped = square[line].T
            rounded = flipped.astype(BF)
            turned[line] = rounded
            rest[line] = (flipped - rounded.astype(F32)).astype(BF)

    for piece_ref, (parts, n_rows) in zip(pieces, layout):
        for part, slot in enumerate(parts):
            first = pl.multiple_of(at_ref[slot], 16)
            panel[pl.ds(first, n_rows), :] = piece_ref[part * n_rows : (part + 1) * n_rows, :]
    unscale = back[:, 0:1] * scale_ref[0]
    last[...] = dot_nn(high[...], wide_ref[...]) + dot_nn(low[...], narrow_ref[...]) * unscale
    for line in range(lines):
        folded[...] = dot_nn(turned[line], panel[...]) + dot_nn(rest[line], panel[...])
        acc = jnp.zeros((8, last.shape[1]), F32)
        for number, group in enumerate(groups):
            block = done[number] if number < len(done) else last
            rows = block.shape[0] // lines
            at = line * rows
            for which in group:
                parts, n_rows = layout[which]
                for slot in parts:
                    first = at_ref[slot]
                    for row in range(0, n_rows, 8):
                        screened = folded[pl.ds(pl.multiple_of(first + row, 8), 8), :]
                        acc += screened * block[at : at + 8, :]
                        at += 8
        out_ref[line : line + 1, :] = jnp.sum(acc, axis=0, keepdims=True)


def close(at, scale, mine, other, wide, narrow, layout, groups, pieces, screens, done, chunk=512):
    rows, aux = mine.shape
    depth = wide.shape[1]
    lines, total = screens[0].shape[0], screens[0].shape[2]
    part = lambda n: pl.BlockSpec((n, chunk), lambda k: (0, k))
    whole = lambda shape: pl.BlockSpec(shape, lambda k: (0,) * len(shape))
    smem = pl.BlockSpec(memory_space=SMEM)
    return pl.pallas_call(
        functools.partial(close_kernel, layout, groups, len(screens)),
        name="close",
        grid=(depth // chunk,),
        in_specs=[smem, smem, whole((rows, aux)), whole((rows, aux)), part(aux), part(aux)]
        + [part(piece.shape[0]) for piece in pieces]
        + [whole(screen.shape) for screen in screens]
        + [part(block.shape[0]) for block in done],
        out_specs=part(lines),
        out_shape=jax.ShapeDtypeStruct((lines, depth), F32),
        scratch_shapes=[
            pltpu.VMEM((rows, aux), BF),
            pltpu.VMEM((rows, aux), F8),
            pltpu.VMEM((rows, TILE), F32),
            pltpu.VMEM((lines, total, total), F32),
            pltpu.VMEM((lines, total, total), BF),
            pltpu.VMEM((lines, total, total), BF),
            pltpu.VMEM((total, chunk), BF),
            pltpu.VMEM((total, chunk), F32),
            pltpu.VMEM((rows, chunk), F32),
        ],
        compiler_params=pltpu.CompilerParams(vmem_limit_bytes=40 << 20),
        cost_estimate=cost(3 * rows * aux * depth + 4 * lines * total * total * depth, 3 * aux * depth + 4 * lines * total * depth),
    )(at, scale, mine, other, wide, narrow, *pieces, *screens, *done)


def body(n_tm, n_aux, factors, panel, weights, tile_mask, forward_table, screening, back_table):
    tm, aux = lax.axis_index("tm"), lax.axis_index("aux")
    block, count = panel.shape[0], screening.shape[0]
    total = block * n_aux
    at_tm = jnp.stack([tm, aux])
    wide, narrow, scale = mask_factors(tile_mask, factors)
    all_weights = [weights] + [swap_with(weights, "tm", step, n_tm) for step in range(1, n_tm)]
    quarter = block // n_tm
    if n_aux == 4 and n_tm == 4 and quarter % 16 == 0:
        near = swap_with(panel, "aux", 1, n_aux)
        mine = lax.dynamic_slice_in_dim(panel, tm * quarter, quarter, 0)
        far = jnp.concatenate([swap_with(mine, "aux", step, n_aux) for step in (2, 3)], axis=0)
        fars = [far] + [swap_with(far, "tm", step, n_tm) for step in (1, 2, 3)]
        pieces = [panel, near] + fars
        slots = [aux ^ step for step in range(n_aux)]
        layout = []
        for step in (0, 1):
            layout.append(((len(slots),), block))
            slots.append((aux ^ step) * block)
        for step in range(n_tm):
            layout.append(((len(slots), len(slots) + 1), quarter))
            slots += [(aux ^ other) * block + (tm ^ step) * quarter for other in (2, 3)]
        groups = [[0], [1, 2], [3, 4, 5]]
        screens = [screening] + [swap_with(screening, "aux", step, n_aux) for step in range(1, n_aux)]
    else:
        full = lax.all_gather(panel, "aux", axis=0, tiled=True)
        cuts = [0, total // 4, total * 5 // 8, total]
        pieces = [full[low:high] for low, high in zip(cuts, cuts[1:])]
        slots = [jnp.zeros_like(tm)] + [jnp.full_like(tm, low) for low in cuts[:-1]]
        layout = [((1 + n,), high - low) for n, (low, high) in enumerate(zip(cuts, cuts[1:]))]
        groups = [[0], [1], [2]]
        screens = [lax.all_gather(screening, "aux", axis=1, tiled=True)]
    at = jnp.stack(slots)
    line_weights = combine(at_tm, forward_table, all_weights, count, 1.0, "weights")
    polars = []
    for number, group in enumerate(groups):
        own = polar(scale, line_weights, [pieces[which] for which in group], wide, narrow, f"polar{number}")
        polars.append((own, swap_with(own, "pair", 1, 2)))
    done = [spread(scale, *polars[n], wide, narrow, f"spread{n}") for n in range(len(groups) - 1)]
    value = close(at, scale, *polars[-1], wide, narrow, tuple(layout), groups, pieces, screens, done)
    if n_aux <= 4:
        value = value + sum(swap_with(value, "aux", step, n_aux) for step in range(1, n_aux))
    else:
        value = lax.psum(value, "aux")
    values = [value] + [swap_with(value, "tm", step, n_tm) for step in range(1, n_tm)]
    return combine(at_tm, back_table, values, weights.shape[0], total ** (-0.5), "sigma")


def solution(mesh):
    placed = (
        P("aux", "pair"),
        P("aux", "pair"),
        P("tm", "pair"),
        P("aux", "pair"),
        P(),
        P("tm", "aux", None),
        P(),
    )
    step = functools.partial(body, mesh.shape["tm"], mesh.shape["aux"])
    return jax.shard_map(step, mesh=mesh, in_specs=placed, out_specs=P("tm", "pair"), check_vma=False)
```

time: 204 us -> 95.3 us (0.47)
  waiting for transfers between devices: 78.7 us -> 12.4 us
  matrix products: 53.9 us -> 0 us
  blocking collectives: 48.5 us -> 0 us
  Pallas kernels: 0 us -> 46.8 us
  starting transfers between devices: 0.12 us -> 29.3 us
  between operations: 13.9 us -> 0.36 us
  other arithmetic: 2.31 us -> 0.09 us
    dot_general x5 -> x0, matrix products: 53.9 us -> none  [the longest x1 25.5 us: body(): jnp.einsum('tpq,qk->tpk', lines_full, masked, precision=highest)]
    pallas_call x0 -> x9, Pallas kernels: none -> 46.8 us  [the longest x3 23.1 us: polar(): pl.pallas_call(functools.partial(polar_kernel, len(pieces)), name=name, g...]
    unnamed x5 -> x0, waiting for transfers between devices: 43.3 us -> none
    all_gather x2 -> x0, waiting for transfers between devices: 35.4 us -> none  [the longest x1 24.9 us: body(): panel_full = lax.all_gather(panel_factors, 'aux', axis=0, tiled=True)]
    ppermute x0 -> x21, starting transfers between devices: none -> 29.3 us  [swap_with(): return lax.ppermute(value, axis, [(at, at ^ step) for at in range(size)])]
    all_gather x2 -> x0, blocking collectives: 28.5 us -> none  [the longest x1 18.2 us: body(): inverse = lax.all_gather(screening, 'aux', axis=1, tiled=True)]
    psum x1 -> x0, blocking collectives: 20 us -> none  [body(): return lax.psum(partial_value, 'aux')]
    ppermute x0 -> x21, waiting for transfers between devices: none -> 12.4 us  [swap_with(): return lax.ppermute(value, axis, [(at, at ^ step) for at in range(size)])]
  transfers between devices with their start and end apart: 4 -> 21, of which waited for: 3 -> 7; matrix products, arithmetic and copies ran while one was open for 1% -> 0% of each run, Pallas kernels for 0% -> 39%
where the time goes in v1:
time: 95.3 us; the launch traced here: 94.9 us
  Pallas kernels  46.8 us (49%)
  starting transfers between devices  29.3 us (31%)
  waiting for transfers between devices  12.4 us (13%)
  local copies, waits for them, and re-layouts  5.98 us (6%)
    ppermute x21, starting transfers between devices, swap_with(): return lax.ppermute(value, axis, [(at, at ^ step) for at in range(size)])  29.3 us
    pallas_call x3, Pallas kernels, polar(): pl.pallas_call(functools.partial(polar_kernel, len(pieces)), name=name, g...  23.1 us
    ppermute x21, waiting for transfers between devices, swap_with(): return lax.ppermute(value, axis, [(at, at ^ step) for at in range(size)])  12.4 us
    pallas_call x2, Pallas kernels, spread(): pl.pallas_call(spread_kernel, name=name, grid=(depth // chunk,), in_specs...  9.71 us
    pallas_call x1, Pallas kernels, close(): pl.pallas_call(functools.partial(close_kernel, layout, groups, len(screen...  8.78 us
    unnamed x39, local copies, waits for them, and re-layouts  4.99 us
    pallas_call x1, Pallas kernels, mask_factors(): pl.pallas_call(mask_kernel, name='mask', in_specs=[smem, vmem], out_specs...  3.09 us
    pallas_call x2, Pallas kernels, combine(): pl.pallas_call(functools.partial(combine_kernel, factor, count), name=nam...  2.1 us
  transfers between devices with their start and end apart: 21, of which 7 were waited for; matrix products, arithmetic and copies ran while one was open for 0% of the time, Pallas kernels for 39%

profile of v1, /device:TPU:0, one launch (start us, length us, event | category | flops | bytes accessed | tf_op | source)
XLA Modules:
  0.0 94.9 jit_solution(13566488356799663083)
XLA Ops:
  0.0 0.9 constant_dynamic-slice_fusion
  0.9 4.1 %collective-permute-start.3 = (bf16[16,2560]{1,0:T(8,128)(2,1)S(1)}, bf16[16,2560]{1,0:T(8,128)(2,1)S(1)}, u32[]{:S(2)}, u32[]{:S(2)}) collective-permute-start(bf16[16,2560]{1,0:T(8,128)(2,1)S(1)} %constant_dynamic-slice_fusion), channel_id=1, source_target_pairs={{0,4},{2,6},{4,0},{6,2},{1,5},{3,7},{5,1},{7,3},{8,12},{10,14},{12... | collective-permute-start | bytes 245768 | tf_op jit(solution)/shard_map/ppermute | solution.py:29
  5.0 1.3 %collective-permute-start.4 = (bf16[16,2560]{1,0:T(8,128)(2,1)S(1)}, bf16[16,2560]{1,0:T(8,128)(2,1)S(1)}, u32[]{:S(2)}, u32[]{:S(2)}) collective-permute-start(bf16[16,2560]{1,0:T(8,128)(2,1)S(1)} %constant_dynamic-slice_fusion), channel_id=1, source_target_pairs={{0,6},{2,4},{4,2},{6,0},{1,7},{3,5},{5,3},{7,1},{8,14},{10,12},{12... | collective-permute-start | bytes 245768 | tf_op jit(solution)/shard_map/ppermute | solution.py:29
  6.3 1.5 %collective-permute-start = (f32[3,2560]{1,0:T(4,128)}, f32[3,2560]{1,0:T(4,128)S(1)}, u32[]{:S(2)}, u32[]{:S(2)}) collective-permute-start(f32[3,2560]{1,0:T(4,128)} %refs_0_.3), channel_id=1, source_target_pairs={{0,8},{8,0},{16,24},{24,16},{1,9},{9,1},{17,25},{25,17},{2,10},{10... | collective-permute-start | bytes 92168 | tf_op jit(solution)/shard_map/ppermute | solution.py:29
  7.8 1.5 %collective-permute-start.1 = (f32[3,2560]{1,0:T(4,128)}, f32[3,2560]{1,0:T(4,128)S(1)}, u32[]{:S(2)}, u32[]{:S(2)}) collective-permute-start(f32[3,2560]{1,0:T(4,128)} %refs_0_.3), channel_id=1, source_target_pairs={{0,16},{8,24},{16,0},{24,8},{1,17},{9,25},{17,1},{25,9},{2,18},{10... | collective-permute-start | bytes 92168 | tf_op jit(solution)/shard_map/ppermute | solution.py:29
  9.3 0.5 collective-permute-start.2
  9.8 1.5 %collective-permute-done.3 = bf16[16,2560]{1,0:T(8,128)(2,1)S(1)} collective-permute-done((bf16[16,2560]{1,0:T(8,128)(2,1)S(1)}, bf16[16,2560]{1,0:T(8,128)(2,1)S(1)}, u32[]{:S(2)}, u32[]{:S(2)}) %collective-permute-start.3) | collective-permute-done | bytes 81952 | tf_op jit(solution)/shard_map/ppermute | solution.py:29
  11.3 0.5 collective-permute-start.9
  11.9 0.0 collective-permute-done.4
  11.9 0.0 copy-start.7
  11.9 1.6 %collective-permute-start.5 = (bf16[32,2560]{1,0:T(8,128)(2,1)S(1)}, bf16[32,2560]{1,0:T(8,128)(2,1)S(1)}, u32[]{:S(2)}, u32[]{:S(2)}) collective-permute-start(bf16[32,2560]{1,0:T(8,128)(2,1)S(1)} %constant_dynamic-update-slice_fusion.refs_1_.refs_2_), channel_id=1, source_target_pairs={{0,8},{8,0},{16,24},{24,16},{1,9},{9,1},{17,25},{25,17},{2,10},{10... | collective-permute-start | bytes 491528 | tf_op jit(solution)/shard_map/ppermute | solution.py:29
  13.4 0.0 collective-permute-done.refs_1_
  13.4 1.5 %collective-permute-start.6 = (bf16[32,2560]{1,0:T(8,128)(2,1)S(1)}, bf16[32,2560]{1,0:T(8,128)(2,1)S(1)}, u32[]{:S(2)}, u32[]{:S(2)}) collective-permute-start(bf16[32,2560]{1,0:T(8,128)(2,1)S(1)} %constant_dynamic-update-slice_fusion.refs_1_.refs_2_), channel_id=1, source_target_pairs={{0,16},{8,24},{16,0},{24,8},{1,17},{9,25},{17,1},{25,9},{2,18},{10... | collective-permute-start | bytes 491528 | tf_op jit(solution)/shard_map/ppermute | solution.py:29
  15.0 0.0 collective-permute-done.1.refs_2_
  15.0 0.5 collective-permute-start.7
  15.4 0.1 pad_add_fusion.at_ref
  15.5 2.1 %copy-done.2 = bf16[768,2560]{1,0:T(8,128)(2,1)S(1)} copy-done((bf16[768,2560]{1,0:T(8,128)(2,1)S(1)}, bf16[768,2560]{1,0:T(8,128)(2,1)}, u32[]{:S(2)}) %copy-start.2) | copy-done | bytes 3932184
  17.6 0.7 copy-done.18
  18.3 3.1 %mask.1 = (bf16[768,2560]{1,0:T(8,128)(2,1)S(1)}, f8e4m3fn[768,2560]{1,0:T(32,128)(4,1)S(1)}, f32[1]{0:T(128)}) custom-call(s32[6,20]{1,0:T(8,128)S(1)} %copy-done.18, bf16[768,2560]{1,0:T(8,128)(2,1)S(1)} %copy-done.2), custom_call_target="tpu_custom_call" | custom-call | flops 7864320 | bytes 9830400 | tf_op jit(solution)/shard_map/mask/pallas_call | solution.py:55
  21.4 0.0 collective-permute-done.2.refs_3_
  21.4 0.0 copy-done.15
  21.4 0.0 copy-done.16
  21.5 0.7 weights.1.weights_ref
  22.2 0.0 collective-permute-done.9.refs_0_.refs_1_
  22.2 8.3 %polar1.1.mine_ref = f32[288,768]{1,0:T(8,128)} custom-call(f32[1]{0:T(128)} %get-tuple-element.8.scale_ref, f32[3,2560]{1,0:T(4,128)S(1)} %weights.1.weights_ref, bf16[64,2560]{1,0:T(8,128)(2,1)S(1)} %collective-permute-done.9.refs_0_.refs_1_, bf16[32,2560]{1,0:T(8,128)(2,1)S(1)} %constant_dynamic-update-slice_fusion.refs_1_.refs_2_, ...), custom_call_target="tpu_custom_call" | custom-call | flops 1698693120 | bytes 6782976 | tf_op jit(solution)/shard_map/polar1/pallas_call | solution.py:138
  30.6 0.0 copy-done.7
  30.6 0.0 collective-permute-start.14
  30.6 0.0 collective-permute-done.5.refs_0_.refs_3_
  30.6 0.0 copy-start.9
  30.6 0.0 collective-permute-done.6.refs_1_.refs_4_
  30.6 0.0 collective-permute-done.7.refs_2_.refs_5_
  30.6 7.6 %polar2.1.mine_ref = f32[288,768]{1,0:T(8,128)S(1)} custom-call(f32[1]{0:T(128)} %get-tuple-element.8.scale_ref, f32[3,2560]{1,0:T(4,128)S(1)} %weights.1.weights_ref, bf16[32,2560]{1,0:T(8,128)(2,1)S(1)} %collective-permute-done.5.refs_0_.refs_3_, bf16[32,2560]{1,0:T(8,128)(2,1)S(1)} %collective-permute-done.6.refs_1_.refs_4_, ...), custom_call_target="tpu_custom_call" | custom-call | flops 1698693120 | bytes 6782976 | tf_op jit(solution)/shard_map/polar2/pallas_call | solution.py:138
  38.2 0.4 collective-permute-start.8
  38.6 7.2 %polar0.1.mine_ref = f32[192,768]{1,0:T(8,128)S(1)} custom-call(f32[1]{0:T(128)} %get-tuple-element.8.scale_ref, f32[3,2560]{1,0:T(4,128)S(1)} %weights.1.weights_ref, bf16[64,2560]{1,0:T(8,128)(2,1)S(1)} %copy-done.3, bf16[768,2560]{1,0:T(8,128)(2,1)S(1)} %get-tuple-element.9.refs_3_.refs_1_.wide_ref.refs_2_, ...), custom_call_target="tpu_custom_call" | custom-call | flops 1132462080 | bytes 6488064 | tf_op jit(solution)/shard_map/polar0/pallas_call | solution.py:138
  45.8 0.3 collective-permute-start.13
  46.1 1.5 %collective-permute-start.10 = (f32[3,64,256]{2,1,0:T(8,128)}, f32[3,64,256]{2,1,0:T(8,128)}, u32[]{:S(2)}, u32[]{:S(2)}) collective-permute-start(f32[3,64,256]{2,1,0:T(8,128)} %refs_6_.1), channel_id=1, source_target_pairs={{0,2},{2,0},{4,6},{6,4},{1,3},{3,1},{5,7},{7,5},{8,10},{10,8},{12,... | collective-permute-start | bytes 589832 | tf_op jit(solution)/shard_map/ppermute | solution.py:29
  47.6 1.9 %collective-permute-start.11 = (f32[3,64,256]{2,1,0:T(8,128)}, f32[3,64,256]{2,1,0:T(8,128)}, u32[]{:S(2)}, u32[]{:S(2)}) collective-permute-start(f32[3,64,256]{2,1,0:T(8,128)} %refs_6_.1), channel_id=1, source_target_pairs={{0,4},{2,6},{4,0},{6,2},{1,5},{3,7},{5,1},{7,3},{8,12},{10,14},{12... | collective-permute-start | bytes 589832 | tf_op jit(solution)/shard_map/ppermute | solution.py:29
  49.5 0.1 stack.68.at_ref
  49.6 0.0 collective-permute-done.13.other_ref
  49.6 1.5 %collective-permute-start.12 = (f32[3,64,256]{2,1,0:T(8,128)}, f32[3,64,256]{2,1,0:T(8,128)S(1)}, u32[]{:S(2)}, u32[]{:S(2)}) collective-permute-start(f32[3,64,256]{2,1,0:T(8,128)} %refs_6_.1), channel_id=1, source_target_pairs={{0,6},{2,4},{4,2},{6,0},{1,7},{3,5},{5,3},{7,1},{8,14},{10,12},{12... | collective-permute-start | bytes 589832 | tf_op jit(solution)/shard_map/ppermute | solution.py:29
  51.2 2.1 %copy-done.1 = bf16[768,2560]{1,0:T(8,128)(2,1)S(1)} copy-done((bf16[768,2560]{1,0:T(8,128)(2,1)S(1)}, bf16[768,2560]{1,0:T(8,128)(2,1)}, u32[]{:S(2)}) %copy-start.1) | copy-done | bytes 3932184
  53.3 4.3 %spread0.1.refs_10_ = f32[192,2560]{1,0:T(8,128)S(1)} custom-call(f32[1]{0:T(128)} %get-tuple-element.8.scale_ref, f32[192,768]{1,0:T(8,128)S(1)} %polar0.1.mine_ref, f32[192,768]{1,0:T(8,128)} %collective-permute-done.13.other_ref, bf16[768,2560]{1,0:T(8,128)(2,1)S(1)} %copy-done.1, ...), custom_call_target="tpu_custom_call" | custom-call | flops 1132462080 | bytes 8454144 | tf_op jit(solution)/shard_map/spread0/pallas_call | solution.py:180
  57.6 0.0 copy-start.4
  57.7 0.0 collective-permute-done.14.other_ref
  57.7 5.4 %spread1.1.refs_11_ = f32[288,2560]{1,0:T(8,128)S(1)} custom-call(f32[1]{0:T(128)} %get-tuple-element.8.scale_ref, f32[288,768]{1,0:T(8,128)} %polar1.1.mine_ref, f32[288,768]{1,0:T(8,128)} %collective-permute-done.14.other_ref, bf16[768,2560]{1,0:T(8,128)(2,1)S(1)} %copy-done.1, f8e4m3fn[768,2560]{1,0:T(32,128)(4,1)S(1)} %get-tuple-element.10.refs_4_.refs_2_.narrow_ref.refs_3_), custom_call_target="tpu_custom_call" | custom-call | flops 1698693120 | bytes 9732096 | tf_op jit(solution)/shard_map/spread1/pallas_call | solution.py:180
  63.1 0.0 copy-start.17
  63.1 0.0 collective-permute-done.10.refs_7_
  63.1 2.0 %collective-permute-done.11.refs_8_ = f32[3,64,256]{2,1,0:T(8,128)} collective-permute-done((f32[3,64,256]{2,1,0:T(8,128)}, f32[3,64,256]{2,1,0:T(8,128)}, u32[]{:S(2)}, u32[]{:S(2)}) %collective-permute-start.11) | collective-permute-done | bytes 196640 | tf_op jit(solution)/shard_map/ppermute | solution.py:29
  65.1 0.0 collective-permute-done.12.refs_9_
  65.1 0.0 collective-permute-done.8.other_ref
  65.1 8.8 %close.1 = f32[3,2560]{1,0:T(4,128)S(1)} custom-call(s32[14]{0:T(128)S(1)} %stack.68.at_ref, f32[1]{0:T(128)} %get-tuple-element.8.scale_ref, f32[288,768]{1,0:T(8,128)S(1)} %polar2.1.mine_ref, f32[288,768]{1,0:T(8,128)} %collective-permute-done.8.other_ref, bf16[768,2560]{1,0:T(8,128)(2,1)} %copy-done, ...), custom_call_target="tpu_custom_call" | custom-call | flops 3711959040 | bytes 13762560 | tf_op jit(solution)/shard_map/close/pallas_call | solution.py:248
  73.9 3.9 %collective-permute-start.15 = (f32[3,2560]{1,0:T(4,128)S(1)}, f32[3,2560]{1,0:T(4,128)S(1)}, u32[]{:S(2)}, u32[]{:S(2)}) collective-permute-start(f32[3,2560]{1,0:T(4,128)S(1)} %close.1), channel_id=1, source_target_pairs={{0,2},{2,0},{4,6},{6,4},{1,3},{3,1},{5,7},{7,5},{8,10},{10,8},{12,... | collective-permute-start | bytes 92168 | tf_op jit(solution)/shard_map/ppermute | solution.py:29
  77.8 1.9 %collective-permute-start.16 = (f32[3,2560]{1,0:T(4,128)S(1)}, f32[3,2560]{1,0:T(4,128)S(1)}, u32[]{:S(2)}, u32[]{:S(2)}) collective-permute-start(f32[3,2560]{1,0:T(4,128)S(1)} %close.1), channel_id=1, source_target_pairs={{0,4},{2,6},{4,0},{6,2},{1,5},{3,7},{5,1},{7,3},{8,12},{10,14},{12... | collective-permute-start | bytes 92168 | tf_op jit(solution)/shard_map/ppermute | solution.py:29
  79.7 1.4 %collective-permute-start.17 = (f32[3,2560]{1,0:T(4,128)S(1)}, f32[3,2560]{1,0:T(4,128)S(1)}, u32[]{:S(2)}, u32[]{:S(2)}) collective-permute-start(f32[3,2560]{1,0:T(4,128)S(1)} %close.1), channel_id=1, source_target_pairs={{0,6},{2,4},{4,2},{6,0},{1,7},{3,5},{5,3},{7,1},{8,14},{10,12},{12... | collective-permute-start | bytes 92168 | tf_op jit(solution)/shard_map/ppermute | solution.py:29
  81.1 0.0 collective-permute-done.15
  81.1 2.2 %collective-permute-done.16 = f32[3,2560]{1,0:T(4,128)S(1)} collective-permute-done((f32[3,2560]{1,0:T(4,128)S(1)}, f32[3,2560]{1,0:T(4,128)S(1)}, u32[]{:S(2)}, u32[]{:S(2)}) %collective-permute-start.16) | collective-permute-done | bytes 30752 | tf_op jit(solution)/shard_map/ppermute | solution.py:29
  83.2 2.3 %collective-permute-done.17 = f32[3,2560]{1,0:T(4,128)S(1)} collective-permute-done((f32[3,2560]{1,0:T(4,128)S(1)}, f32[3,2560]{1,0:T(4,128)S(1)}, u32[]{:S(2)}, u32[]{:S(2)}) %collective-permute-start.17) | collective-permute-done | bytes 30752 | tf_op jit(solution)/shard_map/ppermute | solution.py:29
  85.5 1.6 %collective-permute-start.18 = (f32[3,2560]{1,0:T(4,128)S(1)}, f32[3,2560]{1,0:T(4,128)S(1)}, u32[]{:S(2)}, u32[]{:S(2)}) collective-permute-start(f32[3,2560]{1,0:T(4,128)S(1)} %add_add_fusion.refs_0_), channel_id=1, source_target_pairs={{0,8},{8,0},{16,24},{24,16},{1,9},{9,1},{17,25},{25,17},{2,10},{10... | collective-permute-start | bytes 92168 | tf_op jit(solution)/shard_map/ppermute | solution.py:29
  87.1 1.5 %collective-permute-start.19 = (f32[3,2560]{1,0:T(4,128)S(1)}, f32[3,2560]{1,0:T(4,128)S(1)}, u32[]{:S(2)}, u32[]{:S(2)}) collective-permute-start(f32[3,2560]{1,0:T(4,128)S(1)} %add_add_fusion.refs_0_), channel_id=1, source_target_pairs={{0,16},{8,24},{16,0},{24,8},{1,17},{9,25},{17,1},{25,9},{2,18},{10... | collective-permute-start | bytes 92168 | tf_op jit(solution)/shard_map/ppermute | solution.py:29
  88.6 0.5 collective-permute-start.20
  89.1 0.6 collective-permute-done.18.refs_1_
  89.7 1.4 %collective-permute-done.19.refs_2_ = f32[3,2560]{1,0:T(4,128)S(1)} collective-permute-done((f32[3,2560]{1,0:T(4,128)S(1)}, f32[3,2560]{1,0:T(4,128)S(1)}, u32[]{:S(2)}, u32[]{:S(2)}) %collective-permute-start.19) | collective-permute-done | bytes 30752 | tf_op jit(solution)/shard_map/ppermute | solution.py:29
  91.1 2.4 %collective-permute-done.20.refs_3_ = f32[3,2560]{1,0:T(4,128)S(1)} collective-permute-done((f32[3,2560]{1,0:T(4,128)S(1)}, f32[3,2560]{1,0:T(4,128)S(1)}, u32[]{:S(2)}, u32[]{:S(2)}) %collective-permute-start.20) | collective-permute-done | bytes 30752 | tf_op jit(solution)/shard_map/ppermute | solution.py:29
  93.5 1.4 %sigma.1 = f32[3,2560]{1,0:T(4,128)} custom-call(s32[2]{0:T(128)S(1)} %pad_add_fusion.at_ref, f32[12,12]{1,0:T(8,128)S(1)} %copy-done.17, f32[3,2560]{1,0:T(4,128)S(1)} %add_add_fusion.refs_0_, f32[3,2560]{1,0:T(4,128)S(1)} %collective-permute-done.18.refs_1_, f32[3,2560]{1,0:T(4,128)S(1)} %collective-permute-done.19.refs_2_, ...), custom_call_target="tpu_custom_call" | custom-call | flops 768000 | bytes 153600 | tf_op jit(solution)/shard_map/sigma/pallas_call | solution.py:89
  (31 shorter events, 0.1 us)
Async XLA Ops:
  0.0 21.4 %copy-start.15 = (f32[3,2560]{1,0:T(4,128)S(1)}, f32[3,2560]{1,0:T(4,128)}, u32[]{:S(2)}) copy-start(f32[3,2560]{1,0:T(4,128)} %refs_0_.3) | copy-start | bytes 92164
  0.0 21.4 %copy-start.16 = (f32[12,12]{1,0:T(8,128)S(1)}, f32[12,12]{1,0:T(8,128)}, u32[]{:S(2)}) copy-start(f32[12,12]{1,0:T(8,128)} %table_ref.2) | copy-start | bytes 1732
  0.9 10.4 %collective-permute-start.3 = (bf16[16,2560]{1,0:T(8,128)(2,1)S(1)}, bf16[16,2560]{1,0:T(8,128)(2,1)S(1)}, u32[]{:S(2)}, u32[]{:S(2)}) collective-permute-start(bf16[16,2560]{1,0:T(8,128)(2,1)S(1)} %constant_dynamic-slice_fusion), channel_id=1, source_target_pairs={{0,4},{2,6},{4,0},{6,2},{1,5},{3,7},{5,1},{7,3},{8,12},{10,14},{12... | collective-permute-start | bytes 245768 | tf_op jit(solution)/shard_map/ppermute | solution.py:29
  5.0 6.9 %collective-permute-start.4 = (bf16[16,2560]{1,0:T(8,128)(2,1)S(1)}, bf16[16,2560]{1,0:T(8,128)(2,1)S(1)}, u32[]{:S(2)}, u32[]{:S(2)}) collective-permute-start(bf16[16,2560]{1,0:T(8,128)(2,1)S(1)} %constant_dynamic-slice_fusion), channel_id=1, source_target_pairs={{0,6},{2,4},{4,2},{6,0},{1,7},{3,5},{5,3},{7,1},{8,14},{10,12},{12... | collective-permute-start | bytes 245768 | tf_op jit(solution)/shard_map/ppermute | solution.py:29
  6.3 7.1 %collective-permute-start = (f32[3,2560]{1,0:T(4,128)}, f32[3,2560]{1,0:T(4,128)S(1)}, u32[]{:S(2)}, u32[]{:S(2)}) collective-permute-start(f32[3,2560]{1,0:T(4,128)} %refs_0_.3), channel_id=1, source_target_pairs={{0,8},{8,0},{16,24},{24,16},{1,9},{9,1},{17,25},{25,17},{2,10},{10... | collective-permute-start | bytes 92168 | tf_op jit(solution)/shard_map/ppermute | solution.py:29
  7.8 7.2 %collective-permute-start.1 = (f32[3,2560]{1,0:T(4,128)}, f32[3,2560]{1,0:T(4,128)S(1)}, u32[]{:S(2)}, u32[]{:S(2)}) collective-permute-start(f32[3,2560]{1,0:T(4,128)} %refs_0_.3), channel_id=1, source_target_pairs={{0,16},{8,24},{16,0},{24,8},{1,17},{9,25},{17,1},{25,9},{2,18},{10... | collective-permute-start | bytes 92168 | tf_op jit(solution)/shard_map/ppermute | solution.py:29
  9.3 12.1 %collective-permute-start.2 = (f32[3,2560]{1,0:T(4,128)}, f32[3,2560]{1,0:T(4,128)S(1)}, u32[]{:S(2)}, u32[]{:S(2)}) collective-permute-start(f32[3,2560]{1,0:T(4,128)} %refs_0_.3), channel_id=1, source_target_pairs={{0,24},{8,16},{16,8},{24,0},{1,25},{9,17},{17,9},{25,1},{2,26},{10... | collective-permute-start | bytes 92168 | tf_op jit(solution)/shard_map/ppermute | solution.py:29
  11.3 10.9 %collective-permute-start.9 = (bf16[64,2560]{1,0:T(8,128)(2,1)}, bf16[64,2560]{1,0:T(8,128)(2,1)S(1)}, u32[]{:S(2)}, u32[]{:S(2)}) collective-permute-start(bf16[64,2560]{1,0:T(8,128)(2,1)} %refs_0_.5), channel_id=1, source_target_pairs={{0,2},{2,0},{4,6},{6,4},{1,3},{3,1},{5,7},{7,5},{8,10},{10,8},{12,... | collective-permute-start | bytes 983048 | tf_op jit(solution)/shard_map/ppermute | solution.py:29
  11.9 18.7 %copy-start.7 = (bf16[32,2560]{1,0:T(8,128)(2,1)}, bf16[32,2560]{1,0:T(8,128)(2,1)S(1)}, u32[]{:S(2)}) copy-start(bf16[32,2560]{1,0:T(8,128)(2,1)S(1)} %constant_dynamic-update-slice_fusion.refs_1_.refs_2_) | copy-start | bytes 491524
  11.9 18.7 %collective-permute-start.5 = (bf16[32,2560]{1,0:T(8,128)(2,1)S(1)}, bf16[32,2560]{1,0:T(8,128)(2,1)S(1)}, u32[]{:S(2)}, u32[]{:S(2)}) collective-permute-start(bf16[32,2560]{1,0:T(8,128)(2,1)S(1)} %constant_dynamic-update-slice_fusion.refs_1_.refs_2_), channel_id=1, source_target_pairs={{0,8},{8,0},{16,24},{24,16},{1,9},{9,1},{17,25},{25,17},{2,10},{10... | collective-permute-start | bytes 491528 | tf_op jit(solution)/shard_map/ppermute | solution.py:29
  13.4 17.1 %collective-permute-start.6 = (bf16[32,2560]{1,0:T(8,128)(2,1)S(1)}, bf16[32,2560]{1,0:T(8,128)(2,1)S(1)}, u32[]{:S(2)}, u32[]{:S(2)}) collective-permute-start(bf16[32,2560]{1,0:T(8,128)(2,1)S(1)} %constant_dynamic-update-slice_fusion.refs_1_.refs_2_), channel_id=1, source_target_pairs={{0,16},{8,24},{16,0},{24,8},{1,17},{9,25},{17,1},{25,9},{2,18},{10... | collective-permute-start | bytes 491528 | tf_op jit(solution)/shard_map/ppermute | solution.py:29
  15.0 15.6 %collective-permute-start.7 = (bf16[32,2560]{1,0:T(8,128)(2,1)S(1)}, bf16[32,2560]{1,0:T(8,128)(2,1)S(1)}, u32[]{:S(2)}, u32[]{:S(2)}) collective-permute-start(bf16[32,2560]{1,0:T(8,128)(2,1)S(1)} %constant_dynamic-update-slice_fusion.refs_1_.refs_2_), channel_id=1, source_target_pairs={{0,24},{8,16},{16,8},{24,0},{1,25},{9,17},{17,9},{25,1},{2,26},{10... | collective-permute-start | bytes 491528 | tf_op jit(solution)/shard_map/ppermute | solution.py:29
  15.5 2.1 %copy-start.2 = (bf16[768,2560]{1,0:T(8,128)(2,1)S(1)}, bf16[768,2560]{1,0:T(8,128)(2,1)}, u32[]{:S(2)}) copy-start(bf16[768,2560]{1,0:T(8,128)(2,1)} %factors_ref.1) | copy-start | bytes 11796484
  17.6 0.7 copy-start.18
  21.4 17.2 %copy-start = (bf16[768,2560]{1,0:T(8,128)(2,1)}, bf16[768,2560]{1,0:T(8,128)(2,1)S(1)}, u32[]{:S(2)}) copy-start(bf16[768,2560]{1,0:T(8,128)(2,1)S(1)} %get-tuple-element.9.refs_3_.refs_1_.wide_ref.refs_2_) | copy-start | bytes 11796484
  22.2 8.3 %copy-start.5 = (bf16[64,2560]{1,0:T(8,128)(2,1)}, bf16[64,2560]{1,0:T(8,128)(2,1)S(1)}, u32[]{:S(2)}) copy-start(bf16[64,2560]{1,0:T(8,128)(2,1)S(1)} %collective-permute-done.9.refs_0_.refs_1_) | copy-start | bytes 983044
  30.6 8.0 %copy-start.3 = (bf16[64,2560]{1,0:T(8,128)(2,1)S(1)}, bf16[64,2560]{1,0:T(8,128)(2,1)}, u32[]{:S(2)}) copy-start(bf16[64,2560]{1,0:T(8,128)(2,1)} %refs_0_.5) | copy-start | bytes 983044
  30.6 27.1 %collective-permute-start.14 = (f32[288,768]{1,0:T(8,128)}, f32[288,768]{1,0:T(8,128)}, u32[]{:S(2)}, u32[]{:S(2)}) collective-permute-start(f32[288,768]{1,0:T(8,128)} %polar1.1.mine_ref), channel_id=1, source_target_pairs={{0,1},{1,0},{2,3},{3,2},{4,5},{5,4},{6,7},{7,6},{8,9},{9,8},{10,11... | collective-permute-start | bytes 2654216 | tf_op jit(solution)/shard_map/ppermute | solution.py:29
  30.6 7.6 %copy-start.9 = (bf16[32,2560]{1,0:T(8,128)(2,1)}, bf16[32,2560]{1,0:T(8,128)(2,1)S(1)}, u32[]{:S(2)}) copy-start(bf16[32,2560]{1,0:T(8,128)(2,1)S(1)} %collective-permute-done.5.refs_0_.refs_3_) | copy-start | bytes 491524
  30.6 7.6 %copy-start.11 = (bf16[32,2560]{1,0:T(8,128)(2,1)}, bf16[32,2560]{1,0:T(8,128)(2,1)S(1)}, u32[]{:S(2)}) copy-start(bf16[32,2560]{1,0:T(8,128)(2,1)S(1)} %collective-permute-done.6.refs_1_.refs_4_) | copy-start | bytes 491524
  30.6 7.6 %copy-start.13 = (bf16[32,2560]{1,0:T(8,128)(2,1)}, bf16[32,2560]{1,0:T(8,128)(2,1)S(1)}, u32[]{:S(2)}) copy-start(bf16[32,2560]{1,0:T(8,128)(2,1)S(1)} %collective-permute-done.7.refs_2_.refs_5_) | copy-start | bytes 491524
  38.2 26.9 %collective-permute-start.8 = (f32[288,768]{1,0:T(8,128)S(1)}, f32[288,768]{1,0:T(8,128)}, u32[]{:S(2)}, u32[]{:S(2)}) collective-permute-start(f32[288,768]{1,0:T(8,128)S(1)} %polar2.1.mine_ref), channel_id=1, source_target_pairs={{0,1},{1,0},{2,3},{3,2},{4,5},{5,4},{6,7},{7,6},{8,9},{9,8},{10,11... | collective-permute-start | bytes 2654216 | tf_op jit(solution)/shard_map/ppermute | solution.py:29
  45.8 3.8 %collective-permute-start.13 = (f32[192,768]{1,0:T(8,128)S(1)}, f32[192,768]{1,0:T(8,128)}, u32[]{:S(2)}, u32[]{:S(2)}) collective-permute-start(f32[192,768]{1,0:T(8,128)S(1)} %polar0.1.mine_ref), channel_id=1, source_target_pairs={{0,1},{1,0},{2,3},{3,2},{4,5},{5,4},{6,7},{7,6},{8,9},{9,8},{10,11... | collective-permute-start | bytes 1769480 | tf_op jit(solution)/shard_map/ppermute | solution.py:29
  46.1 17.0 %collective-permute-start.10 = (f32[3,64,256]{2,1,0:T(8,128)}, f32[3,64,256]{2,1,0:T(8,128)}, u32[]{:S(2)}, u32[]{:S(2)}) collective-permute-start(f32[3,64,256]{2,1,0:T(8,128)} %refs_6_.1), channel_id=1, source_target_pairs={{0,2},{2,0},{4,6},{6,4},{1,3},{3,1},{5,7},{7,5},{8,10},{10,8},{12,... | collective-permute-start | bytes 589832 | tf_op jit(solution)/shard_map/ppermute | solution.py:29
  47.6 17.5 %collective-permute-start.11 = (f32[3,64,256]{2,1,0:T(8,128)}, f32[3,64,256]{2,1,0:T(8,128)}, u32[]{:S(2)}, u32[]{:S(2)}) collective-permute-start(f32[3,64,256]{2,1,0:T(8,128)} %refs_6_.1), channel_id=1, source_target_pairs={{0,4},{2,6},{4,0},{6,2},{1,5},{3,7},{5,1},{7,3},{8,12},{10,14},{12... | collective-permute-start | bytes 589832 | tf_op jit(solution)/shard_map/ppermute | solution.py:29
  49.6 15.4 %collective-permute-start.12 = (f32[3,64,256]{2,1,0:T(8,128)}, f32[3,64,256]{2,1,0:T(8,128)S(1)}, u32[]{:S(2)}, u32[]{:S(2)}) collective-permute-start(f32[3,64,256]{2,1,0:T(8,128)} %refs_6_.1), channel_id=1, source_target_pairs={{0,6},{2,4},{4,2},{6,0},{1,7},{3,5},{5,3},{7,1},{8,14},{10,12},{12... | collective-permute-start | bytes 589832 | tf_op jit(solution)/shard_map/ppermute | solution.py:29
  51.2 2.1 %copy-start.1 = (bf16[768,2560]{1,0:T(8,128)(2,1)S(1)}, bf16[768,2560]{1,0:T(8,128)(2,1)}, u32[]{:S(2)}) copy-start(bf16[768,2560]{1,0:T(8,128)(2,1)} %copy-done) | copy-start | bytes 11796484
  57.6 7.5 %copy-start.4 = (bf16[64,2560]{1,0:T(8,128)(2,1)S(1)}, bf16[64,2560]{1,0:T(8,128)(2,1)}, u32[]{:S(2)}) copy-start(bf16[64,2560]{1,0:T(8,128)(2,1)} %refs_0_.5) | copy-start | bytes 983044
  57.6 7.5 %copy-start.6 = (bf16[64,2560]{1,0:T(8,128)(2,1)S(1)}, bf16[64,2560]{1,0:T(8,128)(2,1)}, u32[]{:S(2)}) copy-start(bf16[64,2560]{1,0:T(8,128)(2,1)} %copy-done.5) | copy-start | bytes 983044
  57.6 7.5 %copy-start.8 = (bf16[32,2560]{1,0:T(8,128)(2,1)S(1)}, bf16[32,2560]{1,0:T(8,128)(2,1)}, u32[]{:S(2)}) copy-start(bf16[32,2560]{1,0:T(8,128)(2,1)} %copy-done.7) | copy-start | bytes 491524
  57.6 7.5 %copy-start.10 = (bf16[32,2560]{1,0:T(8,128)(2,1)S(1)}, bf16[32,2560]{1,0:T(8,128)(2,1)}, u32[]{:S(2)}) copy-start(bf16[32,2560]{1,0:T(8,128)(2,1)} %copy-done.9) | copy-start | bytes 491524
  57.7 7.5 %copy-start.12 = (bf16[32,2560]{1,0:T(8,128)(2,1)S(1)}, bf16[32,2560]{1,0:T(8,128)(2,1)}, u32[]{:S(2)}) copy-start(bf16[32,2560]{1,0:T(8,128)(2,1)} %copy-done.11) | copy-start | bytes 491524
  57.7 7.5 %copy-start.14 = (bf16[32,2560]{1,0:T(8,128)(2,1)S(1)}, bf16[32,2560]{1,0:T(8,128)(2,1)}, u32[]{:S(2)}) copy-start(bf16[32,2560]{1,0:T(8,128)(2,1)} %copy-done.13) | copy-start | bytes 491524
  63.1 30.4 %copy-start.17 = (f32[12,12]{1,0:T(8,128)S(1)}, f32[12,12]{1,0:T(8,128)}, u32[]{:S(2)}) copy-start(f32[12,12]{1,0:T(8,128)} %table_ref.3) | copy-start | bytes 1732
  73.9 7.2 %collective-permute-start.15 = (f32[3,2560]{1,0:T(4,128)S(1)}, f32[3,2560]{1,0:T(4,128)S(1)}, u32[]{:S(2)}, u32[]{:S(2)}) collective-permute-start(f32[3,2560]{1,0:T(4,128)S(1)} %close.1), channel_id=1, source_target_pairs={{0,2},{2,0},{4,6},{6,4},{1,3},{3,1},{5,7},{7,5},{8,10},{10,8},{12,... | collective-permute-start | bytes 92168 | tf_op jit(solution)/shard_map/ppermute | solution.py:29
  77.8 5.4 %collective-permute-start.16 = (f32[3,2560]{1,0:T(4,128)S(1)}, f32[3,2560]{1,0:T(4,128)S(1)}, u32[]{:S(2)}, u32[]{:S(2)}) collective-permute-start(f32[3,2560]{1,0:T(4,128)S(1)} %close.1), channel_id=1, source_target_pairs={{0,4},{2,6},{4,0},{6,2},{1,5},{3,7},{5,1},{7,3},{8,12},{10,14},{12... | collective-permute-start | bytes 92168 | tf_op jit(solution)/shard_map/ppermute | solution.py:29
  79.7 5.8 %collective-permute-start.17 = (f32[3,2560]{1,0:T(4,128)S(1)}, f32[3,2560]{1,0:T(4,128)S(1)}, u32[]{:S(2)}, u32[]{:S(2)}) collective-permute-start(f32[3,2560]{1,0:T(4,128)S(1)} %close.1), channel_id=1, source_target_pairs={{0,6},{2,4},{4,2},{6,0},{1,7},{3,5},{5,3},{7,1},{8,14},{10,12},{12... | collective-permute-start | bytes 92168 | tf_op jit(solution)/shard_map/ppermute | solution.py:29
  85.5 4.2 %collective-permute-start.18 = (f32[3,2560]{1,0:T(4,128)S(1)}, f32[3,2560]{1,0:T(4,128)S(1)}, u32[]{:S(2)}, u32[]{:S(2)}) collective-permute-start(f32[3,2560]{1,0:T(4,128)S(1)} %add_add_fusion.refs_0_), channel_id=1, source_target_pairs={{0,8},{8,0},{16,24},{24,16},{1,9},{9,1},{17,25},{25,17},{2,10},{10... | collective-permute-start | bytes 92168 | tf_op jit(solution)/shard_map/ppermute | solution.py:29
  87.1 4.0 %collective-permute-start.19 = (f32[3,2560]{1,0:T(4,128)S(1)}, f32[3,2560]{1,0:T(4,128)S(1)}, u32[]{:S(2)}, u32[]{:S(2)}) collective-permute-start(f32[3,2560]{1,0:T(4,128)S(1)} %add_add_fusion.refs_0_), channel_id=1, source_target_pairs={{0,16},{8,24},{16,0},{24,8},{1,17},{9,25},{17,1},{25,9},{2,18},{10... | collective-permute-start | bytes 92168 | tf_op jit(solution)/shard_map/ppermute | solution.py:29
  88.6 4.9 %collective-permute-start.20 = (f32[3,2560]{1,0:T(4,128)S(1)}, f32[3,2560]{1,0:T(4,128)S(1)}, u32[]{:S(2)}, u32[]{:S(2)}) collective-permute-start(f32[3,2560]{1,0:T(4,128)S(1)} %add_add_fusion.refs_0_), channel_id=1, source_target_pairs={{0,24},{8,16},{16,8},{24,0},{1,25},{9,17},{17,9},{25,1},{2,26},{10... | collective-permute-start | bytes 92168 | tf_op jit(solution)/shard_map/ppermute | solution.py:29
